TPU v7x, 128 devices: a whole 4x4x4 slice. The times are simulated.
128 devices in a mesh: kring: 8 (over y, x_lo), band: 16 (over z, x_hi, core).
Axes of the slice: x: 4 (x_hi: 2, x_lo: 2; x = x_hi * 2 + x_lo), y: 4, z: 4, core: 2. Of those that a mesh axis runs over, the one named last changes fastest.
Arguments:
- current: bfloat16 [262144, 256], P(('kring', 'band')), may hold values from -61 to 61
- previous: bfloat16 [262144, 256], P(('kring', 'band')), may hold values from -6 to 6
- energies: float32 [262144], P(('kring', 'band')), may hold values from 1.5 to 2.5
- targets: int32 [262144], P(('kring', 'band')), may hold values from 0 to 15, as said below
- layer_ids: int32 [327680], P(('kring', 'band')), may hold values from 0 to 1
- conduction_pairs: bfloat16 [327680, 1024], P(('kring', 'band')), may hold values from -0.375 to 0.375
- valence_pairs: bfloat16 [327680, 1024], P(('kring', 'band')), may hold values from -0.228125 to 0.228125
- exchange_pairs: bfloat16 [327680, 1024], P(('kring', 'band')), may hold values from -0.137001939 to 0.137001939
- screened: bfloat16 [8, 2, 1024, 2, 1024], P(None, None, 'band'), may hold values from -0.03203125 to 1.28203125
- coulomb: float32 [2, 2, 1024], replicated, may hold values from 0.2 to 2
- beta_prev: float32 [256], replicated, may hold values from 0.5 to 2
Outputs:
- next_vector: bfloat16 [262144, 256], P(('kring', 'band'))
- lanczos_alpha: float32 [256], replicated
- lanczos_beta: float32 [256], replicated
Inputs may be any that keep to these rules, and one draw needn't show every extreme that they name: `targets`: the 2048 rows of one device name each band index at most 2560 // 16 times; in every k-group one band index is named exactly that often by every device of the group.
All inputs are finite; a program needn't handle non-finite values.
Results may differ from a plain program's by a relative error of at most 0.0057.
Values may be sent and summed in bfloat16 or wider, within the bound.
A program may use at most 128 MiB of HBM per device.

v0:
```python
import jax
import jax.numpy as jnp
from jax import lax
from jax.sharding import PartitionSpec as P

epsilon_mean = 1e-06


def place_rows(targets, capacity, band_count):
    onehot = (targets[:, None] == jnp.arange(band_count, dtype=jnp.int32)[None, :]).astype(
        jnp.int32
    )
    counted = jnp.cumsum(onehot, axis=0)
    ranking = jnp.sum(counted * onehot, axis=1) - 1
    return targets * capacity + ranking


def per_device(
    current,
    previous,
    energies,
    targets,
    layer_ids,
    conduction_pairs,
    valence_pairs,
    exchange_pairs,
    screened,
    coulomb,
    beta_prev,
):
    band_count = lax.axis_size("band")
    own_rows, chains = current.shape
    slot_rows, basis_size = conduction_pairs.shape
    capacity = slot_rows // band_count
    slot_ids = place_rows(targets, capacity, band_count)
    outgoing = jnp.zeros((slot_rows, chains), jnp.bfloat16).at[slot_ids].set(current)
    arrived = lax.all_to_all(
        outgoing.reshape(band_count, capacity, chains),
        "band",
        split_axis=0,
        concat_axis=0,
        tiled=True,
    ).reshape(slot_rows, chains)
    layer_pick = (layer_ids[:, None] == jnp.arange(2, dtype=jnp.int32)[None, :]).astype(
        jnp.bfloat16
    )
    split_amps = arrived[:, None, :] * layer_pick[:, :, None]
    valence_part = jnp.einsum(
        "tg,tln->lgn", valence_pairs, split_amps, preferred_element_type=jnp.float32
    )
    exchange_part = jnp.einsum(
        "tg,tln->lgn", exchange_pairs, split_amps, preferred_element_type=jnp.float32
    )
    projected = lax.psum_scatter(valence_part, "band", scatter_dimension=1, tiled=True).astype(
        jnp.bfloat16
    )
    exchange_total = lax.psum(exchange_part, ("kring", "band"))
    coupled = (
        coulomb[:, 0, :, None] * exchange_total[0][None]
        + coulomb[:, 1, :, None] * exchange_total[1][None]
    ).astype(jnp.bfloat16)
    group_index = lax.axis_index("kring")
    group_count = lax.axis_size("kring")
    pieces = lax.all_gather(projected[None], "kring", axis=0, tiled=True)
    number = pieces.shape[0]
    distance = jnp.mod(group_index - jnp.arange(number, dtype=jnp.int32), group_count)
    blocks = jnp.take(screened, distance, axis=0)
    direct_part = jnp.einsum("kaphg,kapn->hgn", blocks, pieces, preferred_element_type=jnp.float32)
    direct = lax.psum(direct_part, "band").astype(jnp.bfloat16)
    both_direct = jnp.einsum(
        "tg,lgn->tln", conduction_pairs, direct, preferred_element_type=jnp.float32
    )
    both_exchange = jnp.einsum(
        "tg,lgn->tln", exchange_pairs, coupled, preferred_element_type=jnp.float32
    )
    kernel_all = 2.0 * both_exchange - both_direct
    kernel_rows = jnp.sum(kernel_all * layer_pick.astype(jnp.float32)[:, :, None], axis=1).astype(
        jnp.bfloat16
    )
    returned = lax.all_to_all(
        kernel_rows.reshape(band_count, capacity, chains),
        "band",
        split_axis=0,
        concat_axis=0,
        tiled=True,
    ).reshape(slot_rows, chains)
    kernel_own = returned[slot_ids].astype(jnp.float32)
    current_wide = current.astype(jnp.float32)
    applied = energies[:, None] * current_wide + kernel_own
    start_vec = applied - beta_prev[None, :] * previous.astype(jnp.float32)
    total_rows = own_rows * group_count * band_count
    projection, self_norm = lax.psum(
        (jnp.sum(current_wide * start_vec, axis=0), jnp.sum(current_wide * current_wide, axis=0)),
        ("kring", "band"),
    )
    lanczos_alpha = projection / self_norm
    residual = start_vec - lanczos_alpha[None, :] * current_wide
    residual_sq = lax.psum(jnp.sum(residual * residual, axis=0), ("kring", "band"))
    lanczos_beta = jnp.sqrt(residual_sq / total_rows + epsilon_mean)
    next_vector = (residual / lanczos_beta[None, :]).astype(jnp.bfloat16)
    return (next_vector, lanczos_alpha, lanczos_beta)


def solution(mesh):
    in_specs = (
        P(("kring", "band"), None),
        P(("kring", "band"), None),
        P(("kring", "band")),
        P(("kring", "band")),
        P(("kring", "band")),
        P(("kring", "band"), None),
        P(("kring", "band"), None),
        P(("kring", "band"), None),
        P(None, None, "band", None, None),
        P(),
        P(),
    )
    out_specs = (P(("kring", "band"), None), P(), P())
    return jax.shard_map(
        per_device, mesh=mesh, in_specs=in_specs, out_specs=out_specs, check_vma=False
    )
```

profile of v0, /device:TPU:1, one launch (start us, length us, event | category | flops | bytes accessed | tf_op | source)
XLA Modules:
  0.0 529.2 jit_solution(18126593749929816699)
XLA Ops:
  7.2 0.7 fusion.48
  7.9 4.5 reduce-window.6
  12.4 0.4 slice_reduce_fusion
  12.9 0.2 reduce-window.9
  13.0 0.1 broadcast_add_fusion
  13.1 0.0 copy-start.4
  13.2 0.0 copy-start.3
  13.2 0.0 copy-start.8
  13.2 0.8 fusion.47
  13.9 0.7 broadcast_clamp_fusion
  14.7 10.8 %scatter_custom_fusion = bf16[2560,256]{1,0:T(8,128)(2,1)} fusion(s32[2048]{0:T(1024)S(1)} %get-tuple-element.8, bf16[2048,256]{1,0:T(8,128)(2,1)} %param.11, bf16[]{:T(256)} %constant.46.clone.1), kind=kCustom, calls=%fused_computation.44 | custom fusion | bytes 1311232 | tf_op jit(solution)/shard_map/scatter | solution.py:36
  25.5 9.3 %all-to-all-start = ((bf16[16,160,256]{2,1,0:T(8,128)(2,1)}), bf16[16,160,256]{2,1,0:T(8,128)(2,1)S(1)}, u32[]{:S(2)}, u32[]{:S(2)}) async-start(bf16[16,160,256]{2,1,0:T(8,128)(2,1)} %bitcast.2), calls=%async_computation | async-start | bytes 2621440 | tf_op jit(solution)/shard_map/all_to_all | solution.py:37
  34.8 0.2 all-reduce.6.cloned.1.call-start
  35.0 0.0 copy-done.4
  35.1 0.6 dynamic-slice
  36.4 12.0 %gather_fusion = bf16[8,2,64,2,1024]{4,3,2,1,0:T(2,128)(2,1)} fusion(bf16[8,2,64,2,1024]{4,3,2,1,0:T(2,128)(2,1)} %param.19, s32[1024]{0:T(1024)S(1)} %pad_clamp_fusion), kind=kCustom, calls=%fused_computation | custom fusion | bytes 8388640 | tf_op jit(solution)/shard_map/jit(_take)/gather | solution.py:67
  48.4 7.8 %broadcast_select_fusion = bf16[8,2,64,2,1024]{4,3,2,1,0:T(2,128)(2,1)} fusion(bf16[8,2,64,2,1024]{4,3,2,1,0:T(2,128)(2,1)} %gather_fusion, pred[8]{0:T(512)(128)(4,1)S(1)} %compare_and_fusion), kind=kLoop, calls=%fused_computation.3 | loop fusion | flops 2097152 | bytes 8388616 | tf_op jit(solution)/shard_map/jit(_take)/select_n | solution.py:67
  56.2 0.0 all-to-all-done
  56.2 0.8 copy.21
  57.0 6.7 %fusion.28 = f32[2,1024,256]{1,2,0:T(8,128)} fusion(bf16[2560,1024]{1,0:T(8,128)(2,1)} %param.17, bf16[2560,2]{0,1:T(2,128)(2,1)S(1)} %get-tuple-element.10, bf16[2560,256]{0,1:T(8,128)(2,1)S(1)} %copy.21), kind=kOutput, calls=%fused_computation.32 | convolution fusion | flops 2685665280 | bytes 8660992 | tf_op jit(solution)/shard_map/tg,tln->lgn/dot_general | solution.py:48
  63.6 2.8 copy.22
  66.5 84.6 %all-reduce.7 = bf16[2,1024,256]{2,0,1:T(2,128)(2,1)} all-reduce(f32[2,1024,256]{2,0,1:T(2,128)S(1)} %copy.22), channel_id=3, replica_groups=mesh['kring'=8,'band'=16] {'band'}, use_global_device_ids=true, to_apply=%region_5.6.clone | all-reduce | flops 524288 | bytes 3145728
  151.1 0.9 dynamic-slice_convert_fusion
  152.0 0.0 slice-start
  152.0 25.1 %all-gather = bf16[16,64,256]{2,1,0:T(8,128)(2,1)S(1)} all-gather(bf16[2,64,256]{2,1,0:T(8,128)(2,1)S(1)} %copy.23), channel_id=2, replica_groups=mesh['kring'=8,'band'=16] {'kring'}, dimensions={0}, use_global_device_ids=true | all-gather | bytes 589824 | tf_op jit(solution)/shard_map/all_gather | solution.py:64
  177.1 4.3 fusion.20
  181.4 0.0 slice-done
  181.4 0.0 slice-done.1
  181.4 4.3 fusion.23
  185.7 0.0 all-reduce.6.cloned.1.call-update
  185.7 91.2 %all-reduce.8 = bf16[2,1024,256]{2,1,0:T(8,128)(2,1)S(1)} all-reduce(f32[2,1024,256]{2,1,0:T(8,128)S(1)} %fusion.20), channel_id=1, replica_groups=mesh['kring'=8,'band'=16] {'band'}, use_global_device_ids=true, to_apply=%region_6.7 | all-reduce | flops 524288 | bytes 3145728 | tf_op jit(solution)/shard_map/psum | solution.py:69
  277.0 7.3 %fusion.1 = f32[2,256,2560]{2,1,0:T(8,128)} fusion(bf16[2560,1024]{1,0:T(8,128)(2,1)} %param.16, bf16[2,1024,256]{2,1,0:T(8,128)(2,1)S(1)} %all-reduce.8), kind=kOutput, calls=%fused_computation.6 | convolution fusion | flops 2684354560 | bytes 11534336 | tf_op jit(solution)/shard_map/tg,lgn->tln/dot_general | solution.py:70
  284.3 64.9 %all-reduce.6.cloned.1.call-done = f32[2,1024,256]{1,2,0:T(8,128)} async-done(((f32[2,1024,256]{1,2,0:T(8,128)}), f32[2,1024,256]{1,2,0:T(8,128)}) %all-reduce.6.cloned.1.call-update) | async-done | bytes 2097168 | tf_op jit(solution)/shard_map/psum | solution.py:57
  349.2 1.7 slice_bitcast_fusion.1
  350.9 6.9 %fusion = bf16[2560,256]{0,1:T(8,128)(2,1)S(1)} fusion(f32[2,256,2560]{2,1,0:T(8,128)} %fusion.1, bf16[2560,1024]{1,0:T(8,128)(2,1)} %param.18, f32[2560,2]{0,1:T(2,128)S(1)} %get-tuple-element.9, f32[1024,256]{0,1:T(8,128)S(1)} %get-tuple-element.12, f32[2,1024]{1,0:T(2,128)S(1)} %get-tuple-element.15, f32[1024,256]{0,1:T(8,128)S(1)} %get-tuple-element.11, ...), kind=kOutput, calls=%fused_computation.5 | convolution fusion | flops 2691039232 | bytes 13930496 | tf_op jit(solution)/shard_map/tg,lgn->tln/dot_general | solution.py:73
  357.8 0.6 copy.27
  358.4 25.4 %all_to_all.10 = bf16[16,160,256]{2,1,0:T(8,128)(2,1)S(1)} all-to-all(bf16[16,160,256]{2,1,0:T(8,128)(2,1)S(1)} %bitcast.66), channel_id=1, replica_groups=mesh['kring'=8,'band'=16] {'band'}, dimensions={0} | all-to-all | bytes 2621440 | tf_op jit(solution)/shard_map/all_to_all | solution.py:80
  383.8 7.5 %gather_fusion.1 = bf16[2048,256]{1,0:T(8,128)(2,1)S(1)} fusion(bf16[2560,256]{1,0:T(8,128)(2,1)S(1)} %bitcast.64, s32[2048]{0:T(1024)S(1)} %get-tuple-element.7), kind=kCustom, calls=%fused_computation.1 | custom fusion | bytes 2105344 | tf_op jit(solution)/shard_map/gather | solution.py:87
  391.3 0.0 copy-done
  391.3 0.0 copy-done.2
  391.3 0.0 copy-done.5
  391.4 0.0 copy-start.1
  391.4 2.1 fusion.18
  393.5 63.6 %all-reduce.1 = (f32[256]{0:T(256)S(1)}, f32[256]{0:T(256)S(1)}) all-reduce(f32[256]{0:T(256)S(1)} %get-tuple-element.4, f32[256]{0:T(256)S(1)} %get-tuple-element.3), channel_id=1, replica_groups=mesh['kring'=8,'band'=16] {'kring','band'}, use_global_device_ids=true, to_apply=%region_9.10 | all-reduce | flops 512 | bytes 4096 | tf_op jit(solution)/shard_map/psum | solution.py:92
  457.1 0.0 copy-done.1
  457.1 0.8 multiply_reduce_fusion
  457.9 62.7 %psum.39 = f32[256]{0:T(256)S(1)} all-reduce(f32[256]{0:T(256)S(1)} %multiply_reduce_fusion), channel_id=1, replica_groups=mesh['kring'=8,'band'=16] {'kring','band'}, use_global_device_ids=true, to_apply=%region_13.14 | all-reduce | flops 256 | bytes 2048 | tf_op jit(solution)/shard_map/psum | solution.py:98
  520.6 1.7 divide_convert_fusion
  (20 shorter events, 0.1 us)
Async XLA Ops:
  13.1 21.9 %copy-start.4 = (s32[2560]{0:T(1024)S(1)}, s32[2560]{0:T(1024)}, u32[]{:S(2)}) copy-start(s32[2560]{0:T(1024)} %param.15) | copy-start | bytes 30724
  13.2 21.9 %copy-start.3 = (f32[2,2,1024]{2,1,0:T(2,128)S(1)}, f32[2,2,1024]{2,1,0:T(2,128)}, u32[]{:S(2)}) copy-start(f32[2,2,1024]{2,1,0:T(2,128)} %param.20) | copy-start | bytes 49156
  13.2 22.0 %copy-start.8 = (u32[128]{0:T(128)S(1)}, u32[128]{0:T(128)}, u32[]{:S(2)}) copy-start(u32[128]{0:T(128)} %constant.62) | copy-start | bytes 1540
  25.5 30.7 %all-to-all-start = ((bf16[16,160,256]{2,1,0:T(8,128)(2,1)}), bf16[16,160,256]{2,1,0:T(8,128)(2,1)S(1)}, u32[]{:S(2)}, u32[]{:S(2)}) async-start(bf16[16,160,256]{2,1,0:T(8,128)(2,1)} %bitcast.2), calls=%async_computation | async-start | bytes 2621440 | tf_op jit(solution)/shard_map/all_to_all | solution.py:37
  34.8 314.4 %all-reduce.6.cloned.1.call-start = ((), (), s32[]{:S(2)}) async-start(), calls=%async_computation.2 | async-start | bytes 4194304 | tf_op jit(solution)/shard_map/psum | solution.py:57
  152.0 29.4 %slice-start = ((s8[5242880]{0:T(1024)(128)(4,1)}), s8[4194304]{0:T(1024)(128)(4,1)S(1)}, s32[]{:S(2)}) async-start(s8[5242880]{0:T(1024)(128)(4,1)} %bitcast.71), calls=%async_computation.3 | async-start | bytes 8388608
  177.1 4.3 slice-start.1
  383.8 7.5 %copy-start = (bf16[2048,256]{1,0:T(8,128)(2,1)S(1)}, bf16[2048,256]{1,0:T(8,128)(2,1)}, u32[]{:S(2)}) copy-start(bf16[2048,256]{1,0:T(8,128)(2,1)} %param.11) | copy-start | bytes 3145732
  383.8 7.5 %copy-start.2 = (f32[2048]{0:T(1024)S(1)}, f32[2048]{0:T(1024)}, u32[]{:S(2)}) copy-start(f32[2048]{0:T(1024)} %param.13) | copy-start | bytes 24580
  383.8 7.5 %copy-start.5 = (f32[256]{0:T(256)S(1)}, f32[256]{0:T(256)}, u32[]{:S(2)}) copy-start(f32[256]{0:T(256)} %param.21) | copy-start | bytes 3076
  391.4 65.7 %copy-start.1 = (bf16[2048,256]{1,0:T(8,128)(2,1)S(1)}, bf16[2048,256]{1,0:T(8,128)(2,1)}, u32[]{:S(2)}) copy-start(bf16[2048,256]{1,0:T(8,128)(2,1)} %param.12) | copy-start | bytes 3145732
  457.1 65.3 %copy-start.6 = (f32[256]{0:T(256)}, f32[256]{0:T(256)S(1)}, u32[]{:S(2)}) copy-start(f32[256]{0:T(256)S(1)} %div.17) | copy-start | bytes 3076
  520.6 1.8 copy-start.7
Sparse Core Ops, SparseCore 0:
  185.9 163.2 all-reduce.5
where the time goes:
time: 530 us; the launch traced here: 529 us
  blocking collectives  353 us (67%)
  waiting for transfers between devices  64.9 us (12%)
  local copies, waits for them, and re-layouts  38.2 us (7%)
  matrix products  29.5 us (6%)
  other arithmetic  19.5 us (4%)
  between operations  14.9 us (3%)
  starting transfers between devices  9.51 us (2%)
    psum x1, blocking collectives, per_device(): direct = lax.psum(direct_part, 'band').astype(jnp.bfloat16)  91.2 us
    unnamed x1, blocking collectives  84.6 us
    psum x1, waiting for transfers between devices, per_device(): exchange_total = lax.psum(exchange_part, ('kring', 'band'))  64.9 us
    psum x1, blocking collectives, per_device(): lax.psum((jnp.sum(current_wide * start_vec, axis=0), jnp.sum(current_wide...  63.6 us
    psum x1, blocking collectives, per_device(): lax.psum(jnp.sum(residual * residual, axis=0), ('kring', 'band'))  62.7 us
    all_to_all x1, blocking collectives, per_device(): lax.all_to_all(kernel_rows.reshape(band_count, capacity, chains), 'band',...  25.4 us
    all_gather x1, blocking collectives, per_device(): pieces = lax.all_gather(projected[None], 'kring', axis=0, tiled=True)  25.1 us
    gather x1, local copies, waits for them, and re-layouts, per_device(): blocks = jnp.take(screened, distance, axis=0)  12 us
  transfers between devices with their start and end apart: 2, of which 1 were waited for; matrix products, arithmetic and copies ran while one was open for 5% of the time, Pallas kernels for 0%

commit v1 on v0

--- a/solution.py
+++ b/solution.py
@@ -61,7 +61,11 @@
     ).astype(jnp.bfloat16)
     group_index = lax.axis_index("kring")
     group_count = lax.axis_size("kring")
-    pieces = lax.all_gather(projected[None], "kring", axis=0, tiled=True)
+    block = projected[None]
+    size = lax.axis_size("kring")
+    parts = jnp.stack([block for _ in range(size)])
+    parts = lax.all_to_all(parts, "kring", split_axis=0, concat_axis=0)
+    pieces = jnp.concatenate(parts, axis=0)
     number = pieces.shape[0]
     distance = jnp.mod(group_index - jnp.arange(number, dtype=jnp.int32), group_count)
     blocks = jnp.take(screened, distance, axis=0)

time: 530 us -> 506 us (0.955)
  blocking collectives: 353 us -> 324 us
    all_gather x1 -> x0, blocking collectives: 25.1 us -> none  [per_device(): pieces = lax.all_gather(projected[None], 'kring', axis=0, tiled=True)]
  transfers between devices with their start and end apart: 2 -> 3, of which waited for: 1 -> 2; matrix products, arithmetic and copies ran while one was open for 5% -> 8% of each run, Pallas kernels for 0% -> 0%
where the time goes in v1:
time: 506 us; the launch traced here: 505 us
  blocking collectives  324 us (64%)
  waiting for transfers between devices  62.1 us (12%)
  local copies, waits for them, and re-layouts  39.1 us (8%)
  matrix products  31.9 us (6%)
  other arithmetic  19.5 us (4%)
  between operations  14.9 us (3%)
  starting transfers between devices  13.8 us (3%)
    psum x1, blocking collectives, per_device(): direct = lax.psum(direct_part, 'band').astype(jnp.bfloat16)  87.9 us
    unnamed x1, blocking collectives  84.6 us
    psum x1, blocking collectives, per_device(): lax.psum((jnp.sum(current_wide * start_vec, axis=0), jnp.sum(current_wide...  63.6 us
    psum x1, blocking collectives, per_device(): lax.psum(jnp.sum(residual * residual, axis=0), ('kring', 'band'))  62.7 us
    psum x1, waiting for transfers between devices, per_device(): exchange_total = lax.psum(exchange_part, ('kring', 'band'))  61.4 us
    all_to_all x1, blocking collectives, per_device(): lax.all_to_all(kernel_rows.reshape(band_count, capacity, chains), 'band',...  25.4 us
    gather x1, local copies, waits for them, and re-layouts, per_device(): blocks = jnp.take(screened, distance, axis=0)  12 us
    scatter x1, local copies, waits for them, and re-layouts, per_device(): jnp.zeros((slot_rows, chains), jnp.bfloat16).at[slot_ids].set(current)  10.8 us
  transfers between devices with their start and end apart: 3, of which 2 were waited for; matrix products, arithmetic and copies ran while one was open for 8% of the time, Pallas kernels for 0%

profile of v1, /device:TPU:1, one launch (start us, length us, event | category | flops | bytes accessed | tf_op | source)
XLA Modules:
  0.0 505.4 jit_solution(2525513769986910684)
XLA Ops:
  7.2 0.7 fusion.48
  7.9 4.5 reduce-window.6
  12.4 0.4 slice_reduce_fusion
  12.9 0.2 reduce-window.9
  13.0 0.1 broadcast_add_fusion
  13.1 0.0 copy-start.4
  13.2 0.0 copy-start.3
  13.2 0.0 copy-start.8
  13.2 0.8 fusion.47
  13.9 0.7 broadcast_clamp_fusion
  14.7 10.8 %scatter_custom_fusion = bf16[2560,256]{1,0:T(8,128)(2,1)} fusion(s32[2048]{0:T(1024)S(1)} %get-tuple-element.8, bf16[2048,256]{1,0:T(8,128)(2,1)} %param.11, bf16[]{:T(256)} %constant.46.clone.1), kind=kCustom, calls=%fused_computation.44 | custom fusion | bytes 1311232 | tf_op jit(solution)/shard_map/scatter | solution.py:36
  25.5 9.3 %all-to-all-start = ((bf16[16,160,256]{2,1,0:T(8,128)(2,1)}), bf16[16,160,256]{2,1,0:T(8,128)(2,1)S(1)}, u32[]{:S(2)}, u32[]{:S(2)}) async-start(bf16[16,160,256]{2,1,0:T(8,128)(2,1)} %bitcast.2), calls=%async_computation | async-start | bytes 2621440 | tf_op jit(solution)/shard_map/all_to_all | solution.py:37
  34.8 0.0 copy-done.4
  34.9 0.6 dynamic-slice
  36.1 12.0 %gather_fusion = bf16[8,2,64,2,1024]{4,3,2,1,0:T(2,128)(2,1)} fusion(bf16[8,2,64,2,1024]{4,3,2,1,0:T(2,128)(2,1)} %param.19, s32[1024]{0:T(1024)S(1)} %pad_clamp_fusion), kind=kCustom, calls=%fused_computation | custom fusion | bytes 8388640 | tf_op jit(solution)/shard_map/jit(_take)/gather | solution.py:71
  48.2 7.8 %broadcast_select_fusion = bf16[8,2,64,2,1024]{4,3,2,1,0:T(2,128)(2,1)} fusion(bf16[8,2,64,2,1024]{4,3,2,1,0:T(2,128)(2,1)} %gather_fusion, pred[8]{0:T(512)(128)(4,1)S(1)} %compare_and_fusion), kind=kLoop, calls=%fused_computation.3 | loop fusion | flops 2097152 | bytes 8388616 | tf_op jit(solution)/shard_map/jit(_take)/select_n | solution.py:71
  56.0 0.0 all-to-all-done
  56.0 0.8 copy.29
  56.7 6.7 %fusion.28 = f32[2,1024,256]{1,2,0:T(8,128)} fusion(bf16[2560,1024]{1,0:T(8,128)(2,1)} %param.17, bf16[2560,2]{0,1:T(2,128)(2,1)S(1)} %get-tuple-element.10, bf16[2560,256]{0,1:T(8,128)(2,1)S(1)} %copy.29), kind=kOutput, calls=%fused_computation.32 | convolution fusion | flops 2685665280 | bytes 8660992 | tf_op jit(solution)/shard_map/tg,tln->lgn/dot_general | solution.py:48
  63.4 2.8 copy.30
  66.3 84.6 %all-reduce.7 = bf16[2,1024,256]{2,0,1:T(2,128)(2,1)} all-reduce(f32[2,1024,256]{2,0,1:T(2,128)S(1)} %copy.30), channel_id=2, replica_groups=mesh['kring'=8,'band'=16] {'band'}, use_global_device_ids=true, to_apply=%region_5.6.clone | all-reduce | flops 524288 | bytes 3145728
  150.8 0.9 dynamic-slice_convert_fusion
  151.7 0.8 stack.3
  152.6 4.2 all-to-all-start.1
  156.8 0.3 all-reduce.6.cloned.1.call-start
  157.1 6.7 %fusion.23 = f32[2,1024,256]{1,2,0:T(8,128)} fusion(bf16[2560,1024]{1,0:T(8,128)(2,1)} %param.18, bf16[2560,2]{0,1:T(2,128)(2,1)S(1)} %get-tuple-element.10, bf16[2560,256]{0,1:T(8,128)(2,1)S(1)} %copy.29), kind=kOutput, calls=%fused_computation.31 | convolution fusion | flops 2685665280 | bytes 8660992 | tf_op jit(solution)/shard_map/tg,tln->lgn/dot_general | solution.py:51
  163.8 0.0 all-reduce.6.cloned.1.call-update
  163.8 0.6 all-to-all-done.1
  164.4 4.3 fusion.20
  168.8 87.9 %all-reduce.8 = bf16[2,1024,256]{2,1,0:T(8,128)(2,1)S(1)} all-reduce(f32[2,1024,256]{2,1,0:T(8,128)S(1)} %fusion.20), channel_id=1, replica_groups=mesh['kring'=8,'band'=16] {'band'}, use_global_device_ids=true, to_apply=%region_6.7 | all-reduce | flops 524288 | bytes 3145728 | tf_op jit(solution)/shard_map/psum | solution.py:73
  256.6 7.3 %fusion.1 = f32[2,256,2560]{2,1,0:T(8,128)} fusion(bf16[2560,1024]{1,0:T(8,128)(2,1)} %param.16, bf16[2,1024,256]{2,1,0:T(8,128)(2,1)S(1)} %all-reduce.8), kind=kOutput, calls=%fused_computation.6 | convolution fusion | flops 2684354560 | bytes 11534336 | tf_op jit(solution)/shard_map/tg,lgn->tln/dot_general | solution.py:74
  264.0 61.4 %all-reduce.6.cloned.1.call-done = f32[2,1024,256]{1,2,0:T(8,128)} async-done(((f32[2,1024,256]{1,2,0:T(8,128)}), f32[2,1024,256]{1,2,0:T(8,128)}) %all-reduce.6.cloned.1.call-update) | async-done | bytes 2097168 | tf_op jit(solution)/shard_map/psum | solution.py:57
  325.4 1.7 slice_bitcast_fusion.1
  327.1 6.9 %fusion = bf16[2560,256]{0,1:T(8,128)(2,1)S(1)} fusion(f32[2,256,2560]{2,1,0:T(8,128)} %fusion.1, bf16[2560,1024]{1,0:T(8,128)(2,1)} %param.18, f32[2560,2]{0,1:T(2,128)S(1)} %get-tuple-element.9, f32[1024,256]{0,1:T(8,128)S(1)} %get-tuple-element.12, f32[2,1024]{1,0:T(2,128)S(1)} %get-tuple-element.15, f32[1024,256]{0,1:T(8,128)S(1)} %get-tuple-element.11, ...), kind=kOutput, calls=%fused_computation.5 | convolution fusion | flops 2691039232 | bytes 13930496 | tf_op jit(solution)/shard_map/tg,lgn->tln/dot_general | solution.py:77
  334.0 0.6 copy.35
  334.6 25.4 %all_to_all.15 = bf16[16,160,256]{2,1,0:T(8,128)(2,1)S(1)} all-to-all(bf16[16,160,256]{2,1,0:T(8,128)(2,1)S(1)} %bitcast.66), channel_id=1, replica_groups=mesh['kring'=8,'band'=16] {'band'}, dimensions={0} | all-to-all | bytes 2621440 | tf_op jit(solution)/shard_map/all_to_all | solution.py:84
  360.0 7.5 %gather_fusion.1 = bf16[2048,256]{1,0:T(8,128)(2,1)S(1)} fusion(bf16[2560,256]{1,0:T(8,128)(2,1)S(1)} %bitcast.64, s32[2048]{0:T(1024)S(1)} %get-tuple-element.7), kind=kCustom, calls=%fused_computation.1 | custom fusion | bytes 2105344 | tf_op jit(solution)/shard_map/gather | solution.py:91
  367.5 0.0 copy-done
  367.5 0.0 copy-done.2
  367.5 0.0 copy-done.5
  367.5 0.0 copy-start.1
  367.6 2.1 fusion.18
  369.7 63.6 %all-reduce.1 = (f32[256]{0:T(256)S(1)}, f32[256]{0:T(256)S(1)}) all-reduce(f32[256]{0:T(256)S(1)} %get-tuple-element.4, f32[256]{0:T(256)S(1)} %get-tuple-element.3), channel_id=1, replica_groups=mesh['kring'=8,'band'=16] {'kring','band'}, use_global_device_ids=true, to_apply=%region_9.10 | all-reduce | flops 512 | bytes 4096 | tf_op jit(solution)/shard_map/psum | solution.py:96
  433.3 0.0 copy-done.1
  433.3 0.8 multiply_reduce_fusion
  434.1 62.7 %psum.39 = f32[256]{0:T(256)S(1)} all-reduce(f32[256]{0:T(256)S(1)} %multiply_reduce_fusion), channel_id=1, replica_groups=mesh['kring'=8,'band'=16] {'kring','band'}, use_global_device_ids=true, to_apply=%region_13.14 | all-reduce | flops 256 | bytes 2048 | tf_op jit(solution)/shard_map/psum | solution.py:102
  496.8 1.7 divide_convert_fusion
  498.6 0.0 copy-done.6
  (17 shorter events, 0.1 us)
Async XLA Ops:
  13.1 21.7 %copy-start.4 = (s32[2560]{0:T(1024)S(1)}, s32[2560]{0:T(1024)}, u32[]{:S(2)}) copy-start(s32[2560]{0:T(1024)} %param.15) | copy-start | bytes 30724
  13.2 21.7 %copy-start.3 = (f32[2,2,1024]{2,1,0:T(2,128)S(1)}, f32[2,2,1024]{2,1,0:T(2,128)}, u32[]{:S(2)}) copy-start(f32[2,2,1024]{2,1,0:T(2,128)} %param.20) | copy-start | bytes 49156
  13.2 21.7 %copy-start.8 = (u32[128]{0:T(128)S(1)}, u32[128]{0:T(128)}, u32[]{:S(2)}) copy-start(u32[128]{0:T(128)} %constant.62) | copy-start | bytes 1540
  25.5 30.5 %all-to-all-start = ((bf16[16,160,256]{2,1,0:T(8,128)(2,1)}), bf16[16,160,256]{2,1,0:T(8,128)(2,1)S(1)}, u32[]{:S(2)}, u32[]{:S(2)}) async-start(bf16[16,160,256]{2,1,0:T(8,128)(2,1)} %bitcast.2), calls=%async_computation | async-start | bytes 2621440 | tf_op jit(solution)/shard_map/all_to_all | solution.py:37
  152.6 11.9 %all-to-all-start.1 = ((bf16[8,1,2,64,256]{4,3,2,1,0:T(8,128)(2,1)}), bf16[8,1,2,64,256]{4,3,2,1,0:T(8,128)(2,1)}, u32[]{:S(2)}, u32[]{:S(2)}) async-start(bf16[8,1,2,64,256]{4,3,2,1,0:T(8,128)(2,1)} %stack.3), calls=%async_computation.1 | async-start | bytes 1048576 | tf_op jit(solution)/shard_map/all_to_all | solution.py:67
  156.8 168.6 %all-reduce.6.cloned.1.call-start = ((), (), s32[]{:S(2)}) async-start(), calls=%async_computation.3 | async-start | bytes 4194304 | tf_op jit(solution)/shard_map/psum | solution.py:57
  360.0 7.5 %copy-start = (bf16[2048,256]{1,0:T(8,128)(2,1)S(1)}, bf16[2048,256]{1,0:T(8,128)(2,1)}, u32[]{:S(2)}) copy-start(bf16[2048,256]{1,0:T(8,128)(2,1)} %param.11) | copy-start | bytes 3145732
  360.0 7.5 %copy-start.2 = (f32[2048]{0:T(1024)S(1)}, f32[2048]{0:T(1024)}, u32[]{:S(2)}) copy-start(f32[2048]{0:T(1024)} %param.13) | copy-start | bytes 24580
  360.0 7.5 %copy-start.5 = (f32[256]{0:T(256)S(1)}, f32[256]{0:T(256)}, u32[]{:S(2)}) copy-start(f32[256]{0:T(256)} %param.21) | copy-start | bytes 3076
  367.5 65.8 %copy-start.1 = (bf16[2048,256]{1,0:T(8,128)(2,1)S(1)}, bf16[2048,256]{1,0:T(8,128)(2,1)}, u32[]{:S(2)}) copy-start(bf16[2048,256]{1,0:T(8,128)(2,1)} %param.12) | copy-start | bytes 3145732
  433.3 65.3 %copy-start.6 = (f32[256]{0:T(256)}, f32[256]{0:T(256)S(1)}, u32[]{:S(2)}) copy-start(f32[256]{0:T(256)S(1)} %div.17) | copy-start | bytes 3076
  496.8 1.8 copy-start.7
Sparse Core Ops, SparseCore 0:
  164.0 161.3 all-reduce.5
